TPU v7x, 256 devices: a whole 4x4x8 slice. The times are simulated.
256 devices in a mesh: dom: 32 (over x_lo, z, core), kv: 8 (over y, x_hi).
Axes of the slice: x: 4 (x_hi: 2, x_lo: 2; x = x_hi * 2 + x_lo), y: 4, z: 8, core: 2. Of those that a mesh axis runs over, the one named last changes fastest.
Arguments:
- positions: float32 [3, 65536], P(None, ('dom', 'kv')), may hold values from 0 to 60
- features: bfloat16 [65536, 128], P(('dom', 'kv')), may hold values from -6 to 6
- nbr_index: int32 [65536, 64], P(('dom', 'kv')), may hold values from 0 to 4095
- nbr_count: int32 [65536], P(('dom', 'kv')), may hold values from 16 to 64
- nbr_dist: float32 [65536, 64], P(('dom', 'kv')), may hold values from 0.8 to 5
- halo_lists: int32 [32, 2, 1024], P('dom'), may hold values from 0 to 2047
- wave_vectors: float32 [3, 2048], replicated, may hold values from -1.2566371 to 1.2566371, as said below
- w_charge_first: bfloat16 [128, 16], replicated, may hold values from -0.5 to 0.5
- w_long_first: float32 [16, 128], replicated, may hold values from -1.5 to 1.5
- w_value: bfloat16 [128, 128], replicated, may hold values from -0.5 to 0.5
- w_filter: float32 [16, 128], replicated, may hold values from -1.5 to 1.5
- w_charge_second: bfloat16 [128, 16], replicated, may hold values from -0.5 to 0.5
- w_long_second: float32 [16, 128], replicated, may hold values from -1.5 to 1.5
Outputs:
- features_out: bfloat16 [65536, 128], P(('dom', 'kv'))
- forces: float32 [3, 65536], P(None, ('dom', 'kv'))
Inputs may be any that keep to these rules, and one draw needn't show every extreme that they name: `nbr_index`: rows of the atom's own domain table. `nbr_count`: slots at or past the count are padding. `halo_lists`: rows among the domain's own 2048 atoms; repeats may occur. `wave_vectors`: the columns are 2 pi n / 60 for 2048 distinct nonzero integer vectors n of smallest length, no two equal or opposite, in no particular order.
All inputs are finite; a program needn't handle non-finite values.
Results may differ from a plain program's by a relative error of at most 0.0054.
Values may be sent and summed in bfloat16 or wider, within the bound.
No kernel may reach another device: no remote copies, remote signals or barrier semaphores. Data moves between devices by JAX's collectives and lax.ppermute only.
A program may use at most 64 MiB of HBM per device.

v0:
```python
import math
import jax
import jax.numpy as jnp
from jax import lax
from jax.sharding import PartitionSpec as P

HIGHEST_PRECISION = lax.Precision.HIGHEST
LONG_SCALE = 2.0


def passed_along(block, axis, distance):
    devices = range(lax.axis_size(axis))
    route = [((i - distance) % len(devices), i) for i in devices]
    return lax.ppermute(block, axis, route)


def wave_weight(wavevec):
    sq_norm = wavevec[0] * wavevec[0] + wavevec[1] * wavevec[1] + wavevec[2] * wavevec[2]
    return jnp.exp(-0.5 * sq_norm) / (sq_norm + 1.0)


def phase_tables(wavevec, coords):
    phase_angle = (
        wavevec[0][:, None] * coords[0][None, :]
        + wavevec[1][:, None] * coords[1][None, :]
        + wavevec[2][:, None] * coords[2][None, :]
    )
    return (jnp.cos(phase_angle), jnp.sin(phase_angle))


def partial_structure(wavevec, coords, charge):
    cos_table, sin_table = phase_tables(wavevec, coords)
    return (
        jnp.dot(cos_table, charge, precision=HIGHEST_PRECISION, preferred_element_type=jnp.float32),
        jnp.dot(sin_table, charge, precision=HIGHEST_PRECISION, preferred_element_type=jnp.float32),
    )


def partial_project(wavevec, coords, charge, cos_part, sin_part):
    cos_table, sin_table = phase_tables(wavevec, coords)
    weight = wave_weight(wavevec)[:, None]
    cos_weighted = weight * cos_part
    sin_weighted = weight * sin_part
    contract_dims = (((0,), (0,)), ((), ()))
    potential = lax.dot_general(
        cos_table,
        cos_weighted,
        contract_dims,
        precision=HIGHEST_PRECISION,
        preferred_element_type=jnp.float32,
    )
    potential = potential + lax.dot_general(
        sin_table,
        sin_weighted,
        contract_dims,
        precision=HIGHEST_PRECISION,
        preferred_element_type=jnp.float32,
    )
    along_cos = jnp.dot(
        cos_weighted, charge.T, precision=HIGHEST_PRECISION, preferred_element_type=jnp.float32
    )
    along_sin = jnp.dot(
        sin_weighted, charge.T, precision=HIGHEST_PRECISION, preferred_element_type=jnp.float32
    )
    mixed = sin_table * along_cos - cos_table * along_sin
    force = jnp.dot(wavevec, mixed, precision=HIGHEST_PRECISION, preferred_element_type=jnp.float32)
    return (potential, force)


def sliced_range(pos_dom, charge_dom, wave_vectors, total_atoms, atom_dev):
    kv_count = lax.axis_size("kv")
    per_device = wave_vectors.shape[1] // kv_count
    my_waves = lax.dynamic_slice_in_dim(
        wave_vectors, lax.axis_index("kv") * per_device, per_device, 1
    )
    dom_span = pos_dom.shape[1]
    channels = charge_dom.shape[1]
    atom_block = min(512, dom_span)
    block_count = dom_span // atom_block
    coord_blocks = pos_dom.reshape(3, block_count, atom_block).transpose(1, 0, 2)
    charge_blocks = charge_dom.reshape(block_count, atom_block, channels)

    def add_sums(running, member):
        add_cos, add_sin = partial_structure(my_waves, member[0], member[1])
        return ((running[0] + add_cos, running[1] + add_sin), None)

    zero_part = jnp.zeros((per_device, channels), jnp.float32)
    (cos_part, sin_part), _ = lax.scan(
        add_sums, (zero_part, zero_part), (coord_blocks, charge_blocks)
    )
    cos_part, sin_part = lax.psum((cos_part, sin_part), "dom")
    inv_root = 1.0 / math.sqrt(total_atoms)
    cos_part = cos_part * inv_root
    sin_part = sin_part * inv_root
    prefactor = LONG_SCALE / math.sqrt(wave_vectors.shape[1])
    pieces = atom_dev * lax.axis_size("kv") // atom_dev
    coords = pos_dom.reshape(3, pieces, atom_dev).transpose(1, 0, 2)
    charges = charge_dom.reshape(pieces, atom_dev, channels)

    def one_piece(member):
        potential, force = partial_project(my_waves, member[0], member[1], cos_part, sin_part)
        return jnp.concatenate([potential, force.T], axis=1) * prefactor

    summed = lax.psum_scatter(
        lax.map(one_piece, (coords, charges)).reshape(atom_dev * lax.axis_size("kv"), channels + 3),
        "kv",
        scatter_dimension=0,
        tiled=True,
    )
    return (summed[:, :channels], summed[:, channels:].T)


def basis_of(distance, live_count, basis_count):
    centers = 0.5 + 4.5 / (basis_count - 1) * jnp.arange(basis_count, dtype=jnp.int32).astype(
        jnp.float32
    )
    sharpness = ((basis_count - 1) / 4.5) ** 2
    envelope = 0.5 * (jnp.cos(math.pi * distance / 5.0) + 1.0)
    in_list = (
        jnp.arange(distance.shape[1], dtype=jnp.int32)[None, :] < live_count[:, None]
    ).astype(jnp.float32)
    radial = jnp.exp(-sharpness * (distance[..., None] - centers) ** 2)
    return (radial * (envelope * in_list)[..., None]).astype(jnp.bfloat16)


def short_range(hidden, w_value, w_filter, nbr_index, nbr_count, nbr_dist, halo_lists):
    values = jnp.dot(hidden, w_value, preferred_element_type=jnp.float32).astype(jnp.bfloat16)
    v_dom = lax.all_gather(values, "kv", axis=0, tiled=True)
    halo_rows = halo_lists[0]
    from_below = passed_along(v_dom[halo_rows[0]], "dom", 1)
    from_above = passed_along(v_dom[halo_rows[1]], "dom", -1)
    value_table = jnp.concatenate([v_dom, from_below, from_above], axis=0)
    atom_dev = hidden.shape[0]
    neigh_slots = nbr_index.shape[1]
    atom_block = min(64, atom_dev)
    block_count = atom_dev // atom_block

    def one_block(member):
        index_rows, count_rows, dist_rows = member
        picked = value_table[index_rows]
        basis = basis_of(dist_rows, count_rows, w_filter.shape[0])
        contracted = jnp.einsum("ajr,ajf->arf", basis, picked, preferred_element_type=jnp.float32)
        return jnp.einsum("arf,rf->af", contracted, w_filter, precision=HIGHEST_PRECISION)

    message = lax.map(
        one_block,
        (
            nbr_index.reshape(block_count, atom_block, neigh_slots),
            nbr_count.reshape(block_count, atom_block),
            nbr_dist.reshape(block_count, atom_block, neigh_slots),
        ),
    ).reshape(atom_dev, -1)
    return (hidden.astype(jnp.float32) + jax.nn.silu(message)).astype(jnp.bfloat16)


def local(
    positions,
    features,
    nbr_index,
    nbr_count,
    nbr_dist,
    halo_lists,
    wave_vectors,
    w_charge_first,
    w_long_first,
    w_value,
    w_filter,
    w_charge_second,
    w_long_second,
):
    atom_dev = features.shape[0]
    total_atoms = atom_dev * lax.axis_size("dom") * lax.axis_size("kv")
    charge_first = jnp.dot(features, w_charge_first, preferred_element_type=jnp.float32)
    pos_dom, charge_dom = (
        lax.all_gather(positions, "kv", axis=1, tiled=True),
        lax.all_gather(charge_first, "kv", axis=0, tiled=True),
    )
    pot_first, force_first = sliced_range(pos_dom, charge_dom, wave_vectors, total_atoms, atom_dev)
    lifted = jnp.dot(
        pot_first, w_long_first, precision=HIGHEST_PRECISION, preferred_element_type=jnp.float32
    )
    hidden_first = (features.astype(jnp.float32) + jax.nn.silu(lifted)).astype(jnp.bfloat16)
    hidden_second = short_range(
        hidden_first, w_value, w_filter, nbr_index, nbr_count, nbr_dist, halo_lists
    )
    charge_second = jnp.dot(hidden_second, w_charge_second, preferred_element_type=jnp.float32)
    charge_dom = lax.all_gather(charge_second, "kv", axis=0, tiled=True)
    pot_second, force_second = sliced_range(
        pos_dom, charge_dom, wave_vectors, total_atoms, atom_dev
    )
    lifted = jnp.dot(
        pot_second, w_long_second, precision=HIGHEST_PRECISION, preferred_element_type=jnp.float32
    )
    features_out = (hidden_second.astype(jnp.float32) + jax.nn.silu(lifted)).astype(jnp.bfloat16)
    return (features_out, force_first + force_second)


def solution(mesh):
    return jax.shard_map(
        local,
        mesh=mesh,
        in_specs=(
            P(None, ("dom", "kv")),
            P(("dom", "kv"), None),
            P(("dom", "kv"), None),
            P(("dom", "kv")),
            P(("dom", "kv"), None),
            P("dom", None, None),
            P(),
            P(),
            P(),
            P(),
            P(),
            P(),
            P(),
        ),
        out_specs=(P(("dom", "kv"), None), P(None, ("dom", "kv"))),
        check_vma=False,
    )
```

profile of v0, /device:TPU:32, one launch (start us, length us, event | category | flops | bytes accessed | tf_op | source)
XLA Modules:
  0.0 708.0 jit_solution(5735712428069415658)
XLA Ops:
  7.3 34.8 %all_gather.12 = f32[3,2048]{1,0:T(4,128)S(1)} all-gather(f32[3,256]{1,0:T(4,128)} %param.23), channel_id=1, replica_groups=mesh['dom'=32,'kv'=8] {'kv'}, dimensions={1}, use_global_device_ids=true | all-gather | bytes 27648 | tf_op jit(solution)/shard_map/all_gather | solution.py:175
  43.0 34.3 %all_gather.13 = f32[2048,16]{0,1:T(8,128)S(1)} all-gather(f32[256,16]{0,1:T(8,128)S(1)} %fusion.105), channel_id=1, replica_groups=mesh['dom'=32,'kv'=8] {'kv'}, dimensions={0}, use_global_device_ids=true | all-gather | bytes 147456 | tf_op jit(solution)/shard_map/all_gather | solution.py:176
  78.1 19.2 %while.65 = (s32[]{:T(128)}, f32[256,16]{0,1:T(8,128)S(1)}, f32[256,16]{0,1:T(8,128)S(1)}, f32[3,256]{1,0:T(4,128)S(1)}, f32[4,3,512]{2,1,0:T(4,128)S(1)}, /*ind...) while((s32[]{:T(128)}, f32[256,16]{0,1:T(8,128)S(1)}, f32[256,16]{0,1:T(8,128)S(1)}, ...), condition=%wide.region_1.2_spmd.clone, body=%wide.region_0.1_spmd.clone.sunk | while | flops 51658756 | bytes 233624 | solution.py:88
  78.2 2.4 convolution_add_fusion.11
  83.0 2.4 convolution_add_fusion.11
  87.8 2.4 convolution_add_fusion.11
  92.6 2.4 convolution_add_fusion.11
  97.4 103.2 %all-reduce.1 = (f32[256,16]{0,1:T(8,128)S(1)}, f32[256,16]{0,1:T(8,128)S(1)}) all-reduce(f32[256,16]{0,1:T(8,128)S(1)} %get-tuple-element.339, f32[256,16]{0,1:T(8,128)S(1)} %get-tuple-element.340), channel_id=1, replica_groups=mesh['dom'=32,'kv'=8] {'dom'}, use_global_device_ids=true, to_apply=%region_2.3 | all-reduce | flops 8192 | bytes 65536 | tf_op jit(solution)/shard_map/psum | solution.py:91
  201.5 43.6 %while.62 = (s32[]{:T(128)}, f32[8,256,19]{1,0,2:T(8,128)S(1)}, f32[3,256]{1,0:T(4,128)S(1)}, f32[8,3,256]{2,1,0:T(4,128)S(1)}, f32[256,1]{0,1:T(1,128)S(1)}, /*...) while((s32[]{:T(128)}, f32[8,256,19]{1,0,2:T(8,128)S(1)}, ...), condition=%wide.region_5.6_spmd, body=%wide.region_4.5_spmd.sunk | while | flops 54229252 | bytes 1394849 | solution.py:105
  246.0 75.5 %reduce-scatter.3.cloned.1.call-done = f32[256,19]{0,1:T(8,128)} async-done(((f32[2048,19]{0,1:T(8,128)}), f32[256,19]{0,1:T(8,128)}) %reduce-scatter.3.cloned.1.call-update) | async-done | bytes 19472 | tf_op jit(solution)/shard_map/reduce_scatter | solution.py:104
  322.8 36.1 %all_gather.14 = bf16[2048,128]{1,0:T(8,128)(2,1)S(1)} all-gather(bf16[256,128]{1,0:T(8,128)(2,1)S(1)} %convolution_convert_fusion), channel_id=1, replica_groups=mesh['dom'=32,'kv'=8] {'kv'}, dimensions={0}, use_global_device_ids=true | all-gather | bytes 589824 | tf_op jit(solution)/shard_map/all_gather | solution.py:128
  359.0 3.2 gather_fusion.1
  362.5 3.2 gather_fusion.2
  368.3 3.1 collective-permute-done.1
  371.5 51.7 %while.63 = (s32[]{:T(128)}, f32[4,64,128]{2,1,0:T(8,128)S(1)}, f32[4,64,64]{2,1,0:T(8,128)S(1)}, s32[4,64]{1,0:T(4,128)S(1)}, s32[4,64,64]{2,1,0:T(8,128)S(1)},...) while((s32[]{:T(128)}, f32[4,64,128]{2,1,0:T(8,128)S(1)}, ...), condition=%wide.region_8.9_spmd, body=%wide.region_7.8_spmd.sunk | while | flops 17395760 | bytes 3449829 | solution.py:145
  371.8 12.1 %gather_fusion = bf16[4096,128]{1,0:T(8,128)(2,1)S(1)} fusion(bf16[4096,128]{1,0:T(8,128)(2,1)S(1)} %get-tuple-element.930, s32[4096]{0:T(1024)S(1)} %broadcast_clamp_fusion.4), kind=kCustom, calls=%fused_computation.clone.1 | custom fusion | bytes 2113536 | tf_op jit(solution)/shard_map/while/body/eval_jaxpr/gather | solution.py:140
  384.7 12.1 %gather_fusion = bf16[4096,128]{1,0:T(8,128)(2,1)S(1)} fusion(bf16[4096,128]{1,0:T(8,128)(2,1)S(1)} %get-tuple-element.930, s32[4096]{0:T(1024)S(1)} %broadcast_clamp_fusion.4), kind=kCustom, calls=%fused_computation.clone.1 | custom fusion | bytes 2113536 | tf_op jit(solution)/shard_map/while/body/eval_jaxpr/gather | solution.py:140
  397.6 12.1 %gather_fusion = bf16[4096,128]{1,0:T(8,128)(2,1)S(1)} fusion(bf16[4096,128]{1,0:T(8,128)(2,1)S(1)} %get-tuple-element.930, s32[4096]{0:T(1024)S(1)} %broadcast_clamp_fusion.4), kind=kCustom, calls=%fused_computation.clone.1 | custom fusion | bytes 2113536 | tf_op jit(solution)/shard_map/while/body/eval_jaxpr/gather | solution.py:140
  410.5 12.1 %gather_fusion = bf16[4096,128]{1,0:T(8,128)(2,1)S(1)} fusion(bf16[4096,128]{1,0:T(8,128)(2,1)S(1)} %get-tuple-element.930, s32[4096]{0:T(1024)S(1)} %broadcast_clamp_fusion.4), kind=kCustom, calls=%fused_computation.clone.1 | custom fusion | bytes 2113536 | tf_op jit(solution)/shard_map/while/body/eval_jaxpr/gather | solution.py:140
  423.4 34.5 %all_gather.15 = f32[2048,16]{0,1:T(8,128)S(1)} all-gather(f32[256,16]{0,1:T(8,128)S(1)} %fusion.106), channel_id=1, replica_groups=mesh['dom'=32,'kv'=8] {'kv'}, dimensions={0}, use_global_device_ids=true | all-gather | bytes 147456 | tf_op jit(solution)/shard_map/all_gather | solution.py:187
  458.0 19.2 %while.66 = (s32[]{:T(128)}, f32[256,16]{0,1:T(8,128)S(1)}, f32[256,16]{0,1:T(8,128)S(1)}, f32[3,256]{1,0:T(4,128)S(1)}, f32[4,3,512]{2,1,0:T(4,128)S(1)}, /*ind...) while((s32[]{:T(128)}, f32[256,16]{0,1:T(8,128)S(1)}, ...), condition=%wide.region_10.11_spmd.clone, body=%wide.region_9.10_spmd.clone.sunk | while | flops 51658756 | bytes 233624 | solution.py:88
  458.1 2.4 convolution_add_fusion.13
  460.5 2.4 convolution_add_fusion.12
  462.9 2.4 convolution_add_fusion.13
  465.3 2.4 convolution_add_fusion.12
  467.7 2.4 convolution_add_fusion.13
  470.1 2.4 convolution_add_fusion.12
  472.6 2.4 convolution_add_fusion.13
  474.9 2.4 convolution_add_fusion.12
  477.3 102.6 %all-reduce = (f32[256,16]{0,1:T(8,128)S(1)}, f32[256,16]{0,1:T(8,128)S(1)}) all-reduce(f32[256,16]{0,1:T(8,128)S(1)} %get-tuple-element.343, f32[256,16]{0,1:T(8,128)S(1)} %get-tuple-element.344), channel_id=1, replica_groups=mesh['dom'=32,'kv'=8] {'dom'}, use_global_device_ids=true, to_apply=%region_11.12 | all-reduce | flops 8192 | bytes 65536 | tf_op jit(solution)/shard_map/psum | solution.py:91
  580.0 43.6 %while.64 = (s32[]{:T(128)}, f32[8,256,19]{1,0,2:T(8,128)S(1)}, f32[3,256]{1,0:T(4,128)S(1)}, f32[8,3,256]{2,1,0:T(4,128)S(1)}, f32[256,1]{0,1:T(1,128)S(1)}, /*...) while((s32[]{:T(128)}, f32[8,256,19]{1,0,2:T(8,128)S(1)}, ...), condition=%wide.region_14.15_spmd, body=%wide.region_13.14_spmd.sunk | while | flops 54229252 | bytes 1394849 | solution.py:105
  624.4 73.8 %reduce-scatter.5.cloned.1.call-done = f32[256,19]{0,1:T(8,128)} async-done(((f32[2048,19]{0,1:T(8,128)}), f32[256,19]{0,1:T(8,128)}) %reduce-scatter.5.cloned.1.call-update) | async-done | bytes 19472 | tf_op jit(solution)/shard_map/reduce_scatter | solution.py:104
  (313 shorter events, 110.3 us)
Async XLA Ops:
  7.2 315.5 %copy-start = (bf16[128,128]{1,0:T(8,128)(2,1)S(1)}, bf16[128,128]{1,0:T(8,128)(2,1)}, u32[]{:S(2)}) copy-start(bf16[128,128]{1,0:T(8,128)(2,1)} %param.32) | copy-start | bytes 98308
  7.2 314.4 %reduce-scatter.3.cloned.1.call-start = ((), (), s32[]{:S(2)}) async-start(), calls=%async_computation.2 | async-start | bytes 221184 | tf_op jit(solution)/shard_map/reduce_scatter | solution.py:104
  201.5 44.4 %copy-start.4 = (s32[1,2,1024]{2,1,0:T(2,128)S(1)}, s32[1,2,1024]{2,1,0:T(2,128)}, u32[]{:S(2)}) copy-start(s32[1,2,1024]{2,1,0:T(2,128)} %param.28) | copy-start | bytes 24580
  201.5 120.0 %copy-start.3 = (bf16[256,128]{1,0:T(8,128)(2,1)S(1)}, bf16[256,128]{1,0:T(8,128)(2,1)}, u32[]{:S(2)}) copy-start(bf16[256,128]{1,0:T(8,128)(2,1)} %param.24) | copy-start | bytes 196612
  201.5 120.0 %copy-start.7 = (f32[16,128]{1,0:T(8,128)S(1)}, f32[16,128]{1,0:T(8,128)}, u32[]{:S(2)}) copy-start(f32[16,128]{1,0:T(8,128)} %param.31) | copy-start | bytes 24580
  245.9 452.2 %reduce-scatter.5.cloned.1.call-start = ((), (), s32[]{:S(2)}) async-start(), calls=%async_computation.3 | async-start | bytes 221184 | tf_op jit(solution)/shard_map/reduce_scatter | solution.py:104
  362.2 5.3 copy-start.1
  362.2 5.4 copy-start.2
  362.2 5.5 copy-start.6
  362.2 6.1 collective-permute-start
  365.7 5.7 collective-permute-start.1
  367.8 3.7 copy-start.8
  371.5 51.8 %copy-start.5 = (bf16[128,16]{0,1:T(8,128)(2,1)S(1)}, bf16[128,16]{0,1:T(8,128)(2,1)}, u32[]{:S(2)}) copy-start(bf16[128,16]{0,1:T(8,128)(2,1)} %param.34) | copy-start | bytes 12292
  580.0 119.4 %copy-start.9 = (f32[16,128]{1,0:T(8,128)S(1)}, f32[16,128]{1,0:T(8,128)}, u32[]{:S(2)}) copy-start(f32[16,128]{1,0:T(8,128)} %param.35) | copy-start | bytes 24580
Sparse Core Ops, SparseCore 0:
  246.0 75.4 reduce-scatter.2
  624.5 73.5 reduce-scatter.4
where the time goes:
time: 709 us; the launch traced here: 708 us
  blocking collectives  346 us (49%)
  waiting for transfers between devices  153 us (22%)
  matrix products  126 us (18%)
  local copies, waits for them, and re-layouts  61 us (9%)
  between operations  14.4 us (2%)
    psum x2, blocking collectives, sliced_range(): cos_part, sin_part = lax.psum((cos_part, sin_part), 'dom')  206 us
    reduce_scatter x2, waiting for transfers between devices, sliced_range(): lax.psum_scatter(lax.map(one_piece, (coords, charges)).reshape(atom_dev *...  149 us
    gather x4, local copies, waits for them, and re-layouts, one_block(): picked = value_table[index_rows]  48.5 us
    all_gather x1, blocking collectives, short_range(): v_dom = lax.all_gather(values, 'kv', axis=0, tiled=True)  36.1 us
    all_gather x1, blocking collectives, local(): lax.all_gather(positions, 'kv', axis=1, tiled=True)  34.8 us
    all_gather x1, blocking collectives, local(): charge_dom = lax.all_gather(charge_second, 'kv', axis=0, tiled=True)  34.5 us
    all_gather x1, blocking collectives, local(): lax.all_gather(charge_first, 'kv', axis=0, tiled=True)  34.3 us
    dot_general x16, matrix products, partial_project(): jnp.dot(sin_weighted, charge.T, precision=HIGHEST_PRECISION, preferred_el...  20.2 us
  transfers between devices with their start and end apart: 4, of which 4 were waited for; matrix products, arithmetic and copies ran while one was open for 0% of the time, Pallas kernels for 0%

commit v1 on v0

--- a/solution.py
+++ b/solution.py
@@ -125,7 +125,10 @@
 
 def short_range(hidden, w_value, w_filter, nbr_index, nbr_count, nbr_dist, halo_lists):
     values = jnp.dot(hidden, w_value, preferred_element_type=jnp.float32).astype(jnp.bfloat16)
-    v_dom = lax.all_gather(values, "kv", axis=0, tiled=True)
+    size = lax.axis_size("kv")
+    blocks = jnp.stack([values for _ in range(size)])
+    blocks = lax.all_to_all(blocks, "kv", split_axis=0, concat_axis=0)
+    v_dom = jnp.concatenate(blocks, axis=0)
     halo_rows = halo_lists[0]
     from_below = passed_along(v_dom[halo_rows[0]], "dom", 1)
     from_above = passed_along(v_dom[halo_rows[1]], "dom", -1)

time: 709 us -> 687 us (0.969)
  blocking collectives: 346 us -> 310 us
  waiting for transfers between devices: 153 us -> 161 us
    all_gather x1 -> x0, blocking collectives: 36.1 us -> none  [short_range(): v_dom = lax.all_gather(values, 'kv', axis=0, tiled=True)]
    all_to_all x0 -> x1, waiting for transfers between devices: none -> 10.1 us  [short_range(): blocks = lax.all_to_all(blocks, 'kv', split_axis=0, concat_axis=0)]
  transfers between devices with their start and end apart: 4 -> 5, of which waited for: 4 -> 5; matrix products, arithmetic and copies ran while one was open for 0% -> 1% of each run, Pallas kernels for 0% -> 0%
where the time goes in v1:
time: 687 us; the launch traced here: 686 us
  blocking collectives  310 us (45%)
  waiting for transfers between devices  161 us (23%)
  matrix products  126 us (18%)
  local copies, waits for them, and re-layouts  61.9 us (9%)
  between operations  14.4 us (2%)
    psum x2, blocking collectives, sliced_range(): cos_part, sin_part = lax.psum((cos_part, sin_part), 'dom')  206 us
    reduce_scatter x2, waiting for transfers between devices, sliced_range(): lax.psum_scatter(lax.map(one_piece, (coords, charges)).reshape(atom_dev *...  148 us
    gather x4, local copies, waits for them, and re-layouts, one_block(): picked = value_table[index_rows]  48.5 us
    all_gather x1, blocking collectives, local(): lax.all_gather(positions, 'kv', axis=1, tiled=True)  34.8 us
    all_gather x1, blocking collectives, local(): charge_dom = lax.all_gather(charge_second, 'kv', axis=0, tiled=True)  34.5 us
    all_gather x1, blocking collectives, local(): lax.all_gather(charge_first, 'kv', axis=0, tiled=True)  34.3 us
    dot_general x16, matrix products, partial_project(): jnp.dot(sin_weighted, charge.T, precision=HIGHEST_PRECISION, preferred_el...  20.2 us
    dot_general x16, matrix products, partial_project(): jnp.dot(cos_weighted, charge.T, precision=HIGHEST_PRECISION, preferred_el...  20.1 us
  transfers between devices with their start and end apart: 5, of which 5 were waited for; matrix products, arithmetic and copies ran while one was open for 1% of the time, Pallas kernels for 0%

profile of v1, /device:TPU:32, one launch (start us, length us, event | category | flops | bytes accessed | tf_op | source)
XLA Modules:
  0.0 686.0 jit_solution(12406816517072095136)
XLA Ops:
  7.3 34.8 %all_gather.9 = f32[3,2048]{1,0:T(4,128)S(1)} all-gather(f32[3,256]{1,0:T(4,128)} %param.23), channel_id=1, replica_groups=mesh['dom'=32,'kv'=8] {'kv'}, dimensions={1}, use_global_device_ids=true | all-gather | bytes 27648 | tf_op jit(solution)/shard_map/all_gather | solution.py:178
  43.0 34.3 %all_gather.10 = f32[2048,16]{0,1:T(8,128)S(1)} all-gather(f32[256,16]{0,1:T(8,128)S(1)} %fusion.105), channel_id=1, replica_groups=mesh['dom'=32,'kv'=8] {'kv'}, dimensions={0}, use_global_device_ids=true | all-gather | bytes 147456 | tf_op jit(solution)/shard_map/all_gather | solution.py:179
  78.1 19.2 %while.65 = (s32[]{:T(128)}, f32[256,16]{0,1:T(8,128)S(1)}, f32[256,16]{0,1:T(8,128)S(1)}, f32[3,256]{1,0:T(4,128)S(1)}, f32[4,3,512]{2,1,0:T(4,128)S(1)}, /*ind...) while((s32[]{:T(128)}, f32[256,16]{0,1:T(8,128)S(1)}, f32[256,16]{0,1:T(8,128)S(1)}, ...), condition=%wide.region_1.2_spmd.clone, body=%wide.region_0.1_spmd.clone.sunk | while | flops 51658756 | bytes 233624 | solution.py:88
  78.2 2.4 convolution_add_fusion.11
  83.0 2.4 convolution_add_fusion.11
  87.8 2.4 convolution_add_fusion.11
  92.6 2.4 convolution_add_fusion.11
  97.4 103.2 %all-reduce.1 = (f32[256,16]{0,1:T(8,128)S(1)}, f32[256,16]{0,1:T(8,128)S(1)}) all-reduce(f32[256,16]{0,1:T(8,128)S(1)} %get-tuple-element.339, f32[256,16]{0,1:T(8,128)S(1)} %get-tuple-element.340), channel_id=1, replica_groups=mesh['dom'=32,'kv'=8] {'dom'}, use_global_device_ids=true, to_apply=%region_2.3 | all-reduce | flops 8192 | bytes 65536 | tf_op jit(solution)/shard_map/psum | solution.py:91
  201.5 43.6 %while.62 = (s32[]{:T(128)}, f32[8,256,19]{1,0,2:T(8,128)S(1)}, f32[3,256]{1,0:T(4,128)S(1)}, f32[8,3,256]{2,1,0:T(4,128)S(1)}, f32[256,1]{0,1:T(1,128)S(1)}, /*...) while((s32[]{:T(128)}, f32[8,256,19]{1,0,2:T(8,128)S(1)}, ...), condition=%wide.region_5.6_spmd, body=%wide.region_4.5_spmd.sunk | while | flops 54229252 | bytes 1394849 | solution.py:105
  245.9 75.7 %reduce-scatter.3.cloned.1.call-done = f32[256,19]{0,1:T(8,128)} async-done(((f32[2048,19]{0,1:T(8,128)}), f32[256,19]{0,1:T(8,128)}) %reduce-scatter.3.cloned.1.call-update) | async-done | bytes 19472 | tf_op jit(solution)/shard_map/reduce_scatter | solution.py:104
  323.7 4.5 all-to-all-start
  328.4 10.1 %all-to-all-done = bf16[8,256,128]{2,1,0:T(8,128)(2,1)S(1)} async-done(((bf16[8,256,128]{2,1,0:T(8,128)(2,1)}), bf16[8,256,128]{2,1,0:T(8,128)(2,1)S(1)}, u32[]{:S(2)}, u32[]{:S(2)}) %all-to-all-start) | async-done | bytes 524320 | tf_op jit(solution)/shard_map/all_to_all | solution.py:130
  338.5 3.2 gather_fusion.1
  342.0 3.2 gather_fusion.2
  347.8 3.1 collective-permute-done.1
  351.0 51.7 %while.63 = (s32[]{:T(128)}, f32[4,64,128]{2,1,0:T(8,128)S(1)}, f32[4,64,64]{2,1,0:T(8,128)S(1)}, s32[4,64]{1,0:T(4,128)S(1)}, s32[4,64,64]{2,1,0:T(8,128)S(1)},...) while((s32[]{:T(128)}, f32[4,64,128]{2,1,0:T(8,128)S(1)}, ...), condition=%wide.region_8.9_spmd, body=%wide.region_7.8_spmd.sunk | while | flops 17395760 | bytes 3449829 | solution.py:148
  351.3 12.1 %gather_fusion = bf16[4096,128]{1,0:T(8,128)(2,1)S(1)} fusion(bf16[4096,128]{1,0:T(8,128)(2,1)S(1)} %get-tuple-element.930, s32[4096]{0:T(1024)S(1)} %broadcast_clamp_fusion.4), kind=kCustom, calls=%fused_computation.clone.1 | custom fusion | bytes 2113536 | tf_op jit(solution)/shard_map/while/body/eval_jaxpr/gather | solution.py:143
  364.2 12.1 %gather_fusion = bf16[4096,128]{1,0:T(8,128)(2,1)S(1)} fusion(bf16[4096,128]{1,0:T(8,128)(2,1)S(1)} %get-tuple-element.930, s32[4096]{0:T(1024)S(1)} %broadcast_clamp_fusion.4), kind=kCustom, calls=%fused_computation.clone.1 | custom fusion | bytes 2113536 | tf_op jit(solution)/shard_map/while/body/eval_jaxpr/gather | solution.py:143
  377.1 12.1 %gather_fusion = bf16[4096,128]{1,0:T(8,128)(2,1)S(1)} fusion(bf16[4096,128]{1,0:T(8,128)(2,1)S(1)} %get-tuple-element.930, s32[4096]{0:T(1024)S(1)} %broadcast_clamp_fusion.4), kind=kCustom, calls=%fused_computation.clone.1 | custom fusion | bytes 2113536 | tf_op jit(solution)/shard_map/while/body/eval_jaxpr/gather | solution.py:143
  390.0 12.1 %gather_fusion = bf16[4096,128]{1,0:T(8,128)(2,1)S(1)} fusion(bf16[4096,128]{1,0:T(8,128)(2,1)S(1)} %get-tuple-element.930, s32[4096]{0:T(1024)S(1)} %broadcast_clamp_fusion.4), kind=kCustom, calls=%fused_computation.clone.1 | custom fusion | bytes 2113536 | tf_op jit(solution)/shard_map/while/body/eval_jaxpr/gather | solution.py:143
  402.9 34.5 %all_gather.11 = f32[2048,16]{0,1:T(8,128)S(1)} all-gather(f32[256,16]{0,1:T(8,128)S(1)} %fusion.106), channel_id=1, replica_groups=mesh['dom'=32,'kv'=8] {'kv'}, dimensions={0}, use_global_device_ids=true | all-gather | bytes 147456 | tf_op jit(solution)/shard_map/all_gather | solution.py:190
  437.5 19.2 %while.66 = (s32[]{:T(128)}, f32[256,16]{0,1:T(8,128)S(1)}, f32[256,16]{0,1:T(8,128)S(1)}, f32[3,256]{1,0:T(4,128)S(1)}, f32[4,3,512]{2,1,0:T(4,128)S(1)}, /*ind...) while((s32[]{:T(128)}, f32[256,16]{0,1:T(8,128)S(1)}, ...), condition=%wide.region_10.11_spmd.clone, body=%wide.region_9.10_spmd.clone.sunk | while | flops 51658756 | bytes 233624 | solution.py:88
  437.6 2.4 convolution_add_fusion.13
  439.9 2.4 convolution_add_fusion.12
  442.4 2.4 convolution_add_fusion.13
  444.7 2.4 convolution_add_fusion.12
  447.2 2.4 convolution_add_fusion.13
  449.5 2.4 convolution_add_fusion.12
  452.0 2.4 convolution_add_fusion.13
  456.7 102.8 %all-reduce = (f32[256,16]{0,1:T(8,128)S(1)}, f32[256,16]{0,1:T(8,128)S(1)}) all-reduce(f32[256,16]{0,1:T(8,128)S(1)} %get-tuple-element.343, f32[256,16]{0,1:T(8,128)S(1)} %get-tuple-element.344), channel_id=1, replica_groups=mesh['dom'=32,'kv'=8] {'dom'}, use_global_device_ids=true, to_apply=%region_11.12 | all-reduce | flops 8192 | bytes 65536 | tf_op jit(solution)/shard_map/psum | solution.py:91
  559.6 43.6 %while.64 = (s32[]{:T(128)}, f32[8,256,19]{1,0,2:T(8,128)S(1)}, f32[3,256]{1,0:T(4,128)S(1)}, f32[8,3,256]{2,1,0:T(4,128)S(1)}, f32[256,1]{0,1:T(1,128)S(1)}, /*...) while((s32[]{:T(128)}, f32[8,256,19]{1,0,2:T(8,128)S(1)}, ...), condition=%wide.region_14.15_spmd, body=%wide.region_13.14_spmd.sunk | while | flops 54229252 | bytes 1394849 | solution.py:105
  604.0 72.1 %reduce-scatter.5.cloned.1.call-done = f32[256,19]{0,1:T(8,128)} async-done(((f32[2048,19]{0,1:T(8,128)}), f32[256,19]{0,1:T(8,128)}) %reduce-scatter.5.cloned.1.call-update) | async-done | bytes 19472 | tf_op jit(solution)/shard_map/reduce_scatter | solution.py:104
  (315 shorter events, 113.5 us)
Async XLA Ops:
  7.2 315.5 %copy-start = (bf16[128,128]{1,0:T(8,128)(2,1)S(1)}, bf16[128,128]{1,0:T(8,128)(2,1)}, u32[]{:S(2)}) copy-start(bf16[128,128]{1,0:T(8,128)(2,1)} %param.32) | copy-start | bytes 98308
  7.2 314.4 %reduce-scatter.3.cloned.1.call-start = ((), (), s32[]{:S(2)}) async-start(), calls=%async_computation.3 | async-start | bytes 221184 | tf_op jit(solution)/shard_map/reduce_scatter | solution.py:104
  201.5 120.0 %copy-start.3 = (bf16[256,128]{1,0:T(8,128)(2,1)S(1)}, bf16[256,128]{1,0:T(8,128)(2,1)}, u32[]{:S(2)}) copy-start(bf16[256,128]{1,0:T(8,128)(2,1)} %param.24) | copy-start | bytes 196612
  201.5 120.0 %copy-start.7 = (f32[16,128]{1,0:T(8,128)S(1)}, f32[16,128]{1,0:T(8,128)}, u32[]{:S(2)}) copy-start(f32[16,128]{1,0:T(8,128)} %param.31) | copy-start | bytes 24580
  322.7 5.6 copy-start.4
  323.7 14.7 %all-to-all-start = ((bf16[8,256,128]{2,1,0:T(8,128)(2,1)}), bf16[8,256,128]{2,1,0:T(8,128)(2,1)S(1)}, u32[]{:S(2)}, u32[]{:S(2)}) async-start(bf16[8,256,128]{2,1,0:T(8,128)(2,1)} %stack.2), calls=%async_computation.1 | async-start | bytes 1048576 | tf_op jit(solution)/shard_map/all_to_all | solution.py:130
  328.3 347.8 %reduce-scatter.5.cloned.1.call-start = ((), (), s32[]{:S(2)}) async-start(), calls=%async_computation.4 | async-start | bytes 221184 | tf_op jit(solution)/shard_map/reduce_scatter | solution.py:104
  341.7 5.3 copy-start.1
  341.7 5.4 copy-start.2
  341.7 5.5 copy-start.6
  341.7 6.1 collective-permute-start
  345.2 5.7 collective-permute-start.1
  347.3 3.7 copy-start.8
  351.0 51.8 %copy-start.5 = (bf16[128,16]{0,1:T(8,128)(2,1)S(1)}, bf16[128,16]{0,1:T(8,128)(2,1)}, u32[]{:S(2)}) copy-start(bf16[128,16]{0,1:T(8,128)(2,1)} %param.34) | copy-start | bytes 12292
  559.6 117.8 %copy-start.9 = (f32[16,128]{1,0:T(8,128)S(1)}, f32[16,128]{1,0:T(8,128)}, u32[]{:S(2)}) copy-start(f32[16,128]{1,0:T(8,128)} %param.35) | copy-start | bytes 24580
Sparse Core Ops, SparseCore 0:
  246.0 75.5 reduce-scatter.2
  604.1 71.9 reduce-scatter.4
